TPU v7x, 256 devices: a whole 4x4x8 slice. The times are simulated.
256 devices in a mesh: seq: 16 (over z, core), dp: 16 (over y, x).
Axes of the slice: x: 4, y: 4, z: 8, core: 2. Of those that a mesh axis runs over, the one named last changes fastest.
Arguments:
- queries: bfloat16 [16, 2048, 1280], P('dp', 'seq'), may hold values from -43 to 43
- key_rows: bfloat16 [16, 2048, 1280], P('dp', 'seq'), may hold values from -7 to 7
- value_rows: bfloat16 [16, 2048, 1280], P('dp', 'seq'), may hold values from -6 to 6
- resid_in: bfloat16 [16, 2048, 1280], P('dp', 'seq'), may hold values from -6 to 6
- llm_grad: bfloat16 [16, 3072, 1280], P('dp', 'seq'), may hold values from -6 to 6
- vision_slot: int32 [16, 3072], P('dp', 'seq'), may hold values from -1 to 2047, as said below
- window_mask: int32 [16, 32, 2], P('dp', 'seq'), may hold values from 0 to 1, as said below
- w_up: bfloat16 [1280, 2560], P('dp'), may hold values from -0.15625 to 0.15625
- w_down: bfloat16 [2560, 1280], P('dp'), may hold values from -0.125 to 0.125
- norm_gain: bfloat16 [1280], P('dp'), may hold values from 0.25 to 1.75
Outputs:
- grad_query: bfloat16 [16, 2048, 1280], P('dp', 'seq')
- grad_key: bfloat16 [16, 2048, 1280], P('dp', 'seq')
- grad_value: bfloat16 [16, 2048, 1280], P('dp', 'seq')
- grad_resid: bfloat16 [16, 2048, 1280], P('dp', 'seq')
- grad_up: bfloat16 [1280, 2560], P('seq', 'dp')
- grad_down: bfloat16 [2560, 1280], P('seq', 'dp')
- grad_gain: float32 [1280], replicated
Inputs may be any that keep to these rules, and one draw needn't show every extreme that they name: `vision_slot`: -1 marks a text position; every vision token of a batch stands at exactly one position. Positions come in aligned runs of 16: each run is text or the 16 consecutive vision tokens of one tile, in order. Each language-model shard holds exactly 8 tiles, and at most 32 vision tokens of one owner; in every batch, for every owner, some shard holds exactly 32 of that owner's vision tokens. `window_mask`: each owner's 2 blocks are split into images of one or more consecutive blocks; a block attends to exactly the blocks of its own image, itself included (entry i % 2 of row i is 1).
All inputs are finite; a program needn't handle non-finite values.
Results may differ from a plain program's by a relative error of at most 0.023.
Values may be sent and summed in bfloat16 or wider, within the bound.
A program may use at most 128 MiB of HBM per device.

v0:
```python
import math
import jax
import jax.numpy as jnp
from jax import lax
from jax.sharding import PartitionSpec as P

HEADS = 16
HDIM = 80
BLK = 64
PIECE = 16


def contract(left, right, left_dim, right_dim):
    return lax.dot_general(
        left, right, (((left_dim,), (right_dim,)), ((), ())), preferred_element_type=jnp.float32
    )


def per_device(
    queries,
    key_rows,
    value_rows,
    resid_in,
    llm_grad,
    vision_slot,
    window_mask,
    w_up,
    w_down,
    norm_gain,
):
    seq_count = lax.axis_size("seq")
    data_count = lax.axis_size("dp")
    query = queries[0]
    key_block = key_rows[0]
    value_block = value_rows[0]
    tokens, feat_dim = query.shape
    att_scale = 1.0 / math.sqrt(HDIM)
    up_full, down_full, gain_full = (
        lax.all_gather(w_up, "dp", axis=0, tiled=True),
        lax.all_gather(w_down, "dp", axis=0, tiled=True),
        lax.all_gather(norm_gain, "dp", axis=0, tiled=True),
    )
    slot_ids = vision_slot[0]
    piece_count = tokens // PIECE
    capacity = PIECE * (1 + (piece_count + seq_count - 2) // seq_count)
    owner_of = jnp.where(slot_ids >= 0, slot_ids // tokens, seq_count)
    onehot = (owner_of[:, None] == jnp.arange(seq_count)[None, :]).astype(jnp.int32)
    ranking = jnp.sum((jnp.cumsum(onehot, axis=0) - 1) * onehot, axis=1)
    target = jnp.where(slot_ids >= 0, owner_of * capacity + ranking, seq_count * capacity)
    send_rows = (
        jnp.zeros((seq_count * capacity, feat_dim), jnp.bfloat16)
        .at[target]
        .set(llm_grad[0], mode="drop")
    )
    send_ids = (
        jnp.full((seq_count * capacity,), -1, jnp.int32)
        .at[target]
        .set(jnp.where(slot_ids >= 0, slot_ids % tokens, -1), mode="drop")
    )
    recv_rows = lax.all_to_all(
        send_rows.reshape(seq_count, capacity, feat_dim),
        "seq",
        split_axis=0,
        concat_axis=0,
        tiled=True,
    )
    recv_ids = lax.all_to_all(
        send_ids.reshape(seq_count, capacity), "seq", split_axis=0, concat_axis=0, tiled=True
    )
    flat_ids = recv_ids.reshape(seq_count * capacity)
    landing = jnp.where(flat_ids >= 0, flat_ids, tokens)
    grad_rows = (
        jnp.zeros((tokens, feat_dim), jnp.bfloat16)
        .at[landing]
        .set(recv_rows.reshape(seq_count * capacity, feat_dim), mode="drop")
    )
    allowed = jnp.repeat(jnp.repeat(window_mask[0] > 0, BLK, axis=0), BLK, axis=1)
    q_heads = query.reshape(tokens, HEADS, HDIM)
    k_heads = key_block.reshape(tokens, HEADS, HDIM)
    v_heads = value_block.reshape(tokens, HEADS, HDIM)
    scores = (
        jnp.einsum("qhd,khd->hqk", q_heads, k_heads, preferred_element_type=jnp.float32) * att_scale
    )
    masked = jnp.where(allowed[None], scores, -jnp.inf)
    highest = jnp.max(masked, axis=2, keepdims=True)
    exp_terms = jnp.where(allowed[None], jnp.exp(masked - highest), 0.0)
    attn_probs = exp_terms / jnp.sum(exp_terms, axis=2, keepdims=True)
    probs_low = attn_probs.astype(jnp.bfloat16)
    attn_heads = jnp.einsum(
        "hqk,khd->qhd", probs_low, v_heads, preferred_element_type=jnp.float32
    ).astype(jnp.bfloat16)
    attn_out = attn_heads.reshape(tokens, feat_dim)
    hidden = resid_in[0].astype(jnp.float32) + attn_out.astype(jnp.float32)
    center = jnp.mean(hidden, axis=1, keepdims=True)
    variance = jnp.mean(jnp.square(hidden - center), axis=1, keepdims=True)
    inverse = lax.rsqrt(variance + 1e-06)
    normal_unit = (hidden - center) * inverse
    gain_wide = gain_full.astype(jnp.float32)
    normed = (normal_unit * gain_wide).astype(jnp.bfloat16)
    pre_act = jnp.dot(normed, up_full, preferred_element_type=jnp.float32)
    sig_gate = jax.nn.sigmoid(1.702 * pre_act)
    act_low = (pre_act * sig_gate).astype(jnp.bfloat16)
    down_term = contract(act_low, grad_rows, 0, 0)
    d_act = contract(grad_rows, down_full, 1, 1)
    d_pre = (d_act * (sig_gate + 1.702 * pre_act * sig_gate * (1.0 - sig_gate))).astype(
        jnp.bfloat16
    )
    d_normed = contract(d_pre, up_full, 1, 1)
    gain_term = jnp.sum(d_normed * normal_unit, axis=0)
    d_unit = d_normed * gain_wide
    d_hidden = inverse * (
        d_unit
        - jnp.mean(d_unit, axis=1, keepdims=True)
        - normal_unit * jnp.mean(d_unit * normal_unit, axis=1, keepdims=True)
    )
    grad_resid = (grad_rows.astype(jnp.float32) + d_hidden).astype(jnp.bfloat16)
    up_term = contract(normed, d_pre, 0, 0)
    grad_heads = grad_resid.reshape(tokens, HEADS, HDIM)
    grad_value = jnp.einsum(
        "hqk,qhd->khd", probs_low, grad_heads, preferred_element_type=jnp.float32
    ).astype(jnp.bfloat16)
    d_probs = jnp.einsum("qhd,khd->hqk", grad_heads, v_heads, preferred_element_type=jnp.float32)
    delta = jnp.einsum("qhd,qhd->hq", grad_heads, attn_heads, preferred_element_type=jnp.float32)
    d_scores = (attn_probs * (d_probs - delta[:, :, None]) * att_scale).astype(jnp.bfloat16)
    grad_query = jnp.einsum(
        "hqk,khd->qhd", d_scores, k_heads, preferred_element_type=jnp.float32
    ).astype(jnp.bfloat16)
    grad_key = jnp.einsum(
        "hqk,qhd->khd", d_scores, q_heads, preferred_element_type=jnp.float32
    ).astype(jnp.bfloat16)
    up_part, down_part = (
        lax.psum_scatter(
            up_term.astype(jnp.bfloat16), "seq", scatter_dimension=0, tiled=True
        ).astype(jnp.float32),
        lax.psum_scatter(
            down_term.astype(jnp.bfloat16), "seq", scatter_dimension=0, tiled=True
        ).astype(jnp.float32),
    )
    up_panel, down_panel = (
        lax.psum_scatter(
            up_part.astype(jnp.bfloat16), "dp", scatter_dimension=1, tiled=True
        ).astype(jnp.float32),
        lax.psum_scatter(
            down_part.astype(jnp.bfloat16), "dp", scatter_dimension=1, tiled=True
        ).astype(jnp.float32),
    )
    factor = 1.0 / math.sqrt(data_count * seq_count * tokens)
    gain_total = lax.psum(gain_term, ("seq", "dp"))
    return (
        grad_query.reshape(1, tokens, feat_dim),
        grad_key.reshape(1, tokens, feat_dim),
        grad_value.reshape(1, tokens, feat_dim),
        grad_resid[None],
        (up_panel * factor).astype(jnp.bfloat16),
        (down_panel * factor).astype(jnp.bfloat16),
        gain_total * factor,
    )


def solution(mesh):
    in_specs = (
        P("dp", "seq", None),
        P("dp", "seq", None),
        P("dp", "seq", None),
        P("dp", "seq", None),
        P("dp", "seq", None),
        P("dp", "seq"),
        P("dp", "seq", None),
        P("dp", None),
        P("dp", None),
        P("dp"),
    )
    out_specs = (
        P("dp", "seq", None),
        P("dp", "seq", None),
        P("dp", "seq", None),
        P("dp", "seq", None),
        P("seq", "dp"),
        P("seq", "dp"),
        P(),
    )
    return jax.shard_map(
        per_device, mesh=mesh, in_specs=in_specs, out_specs=out_specs, check_vma=False
    )
```

profile of v0, /device:TPU:2, one launch (start us, length us, event | category | flops | bytes accessed | tf_op | source)
XLA Modules:
  0.0 466.7 jit_solution(10220901300629912734)
XLA Ops:
  11.0 1.2 scatter_custom_fusion
  12.9 8.6 %all-to-all-start = ((s32[16,1,32]{2,1,0:T(1,128)}), s32[16,1,32]{2,1,0:T(1,128)S(1)}, u32[]{:S(2)}, u32[]{:S(2)}) async-start(s32[16,1,32]{2,1,0:T(1,128)} %all_to_all.9), calls=%async_computation | async-start | bytes 16384 | tf_op jit(solution)/shard_map/all_to_all | solution.py:67
  21.5 2.7 scatter_custom_fusion.1
  24.1 4.9 %all-to-all-done = s32[16,1,32]{2,1,0:T(1,128)S(1)} async-done(((s32[16,1,32]{2,1,0:T(1,128)}), s32[16,1,32]{2,1,0:T(1,128)S(1)}, u32[]{:S(2)}, u32[]{:S(2)}) %all-to-all-start) | async-done | bytes 2080 | tf_op jit(solution)/shard_map/all_to_all | solution.py:67
  29.0 3.8 all-to-all-start.1
  34.4 1.5 fusion.35
  35.9 1.6 convolution_convert_fusion.3
  40.4 37.7 %all-reduce.1 = bf16[1280]{0:T(1024)(128)(2,1)S(1)} all-reduce(bf16[1280]{0:T(1024)(128)(2,1)S(1)} %dynamic-update-slice), channel_id=1, replica_groups=mesh['seq'=16,'dp'=16] {'dp'}, use_global_device_ids=true, to_apply=%add.1 | all-reduce | flops 1280 | bytes 5120
  79.7 2.9 scatter_custom_fusion.2
  82.7 3.9 fusion.31
  86.6 64.3 %all-gather.3.cloned.1.call-done = bf16[2560,1280]{1,0:T(8,128)(2,1)} async-done(((bf16[160,1280]{1,0:T(8,128)(2,1)}), bf16[2560,1280]{1,0:T(8,128)(2,1)}) %all-gather.3.cloned.1.call-update) | async-done | bytes 6553616 | tf_op jit(solution)/shard_map/all_gather | solution.py:40
  151.0 5.1 %fusion.1 = bf16[128,2560]{1,0:T(8,128)(2,1)S(1)} fusion(bf16[128,1280]{1,0:T(8,128)(2,1)S(1)} %scatter_custom_fusion.2, bf16[2560,1280]{1,0:T(8,128)(2,1)} %all-gather.3.cloned.1.call-done, f32[128,2560]{1,0:T(8,128)S(1)} %fusion.31), kind=kOutput, calls=%fused_computation.7 | convolution fusion | flops 842137600 | bytes 8847360 | tf_op jit(solution)/shard_map/dot_general | solution.py:14
  156.1 4.7 convolution_convert_fusion.1
  160.8 4.6 convolution_convert_fusion
  165.5 5.2 %multiply_reduce_fusion = (f32[1280]{0:T(1024)S(1)}, f32[128]{0:T(128)S(1)}, f32[128]{0:T(128)S(1)}, f32[128,1280]{1,0:T(8,128)S(1)}) fusion(f32[128,1280]{1,0:T(8,128)S(1)} %get-tuple-element.32, f32[128]{0:T(128)S(1)} %add_rsqrt_fusion, f32[128]{0:T(128)S(1)} %broadcast_multiply_fusion.3, f32[1280]{0:T(1024)S(1)} %convert_element_type.92, ...), kind=kOutput, calls=%fused_computation.26 | convolution fusion | flops 840169984 | bytes 8531968 | tf_op jit(solution)/shard_map/dot_general | solution.py:14
  170.7 57.6 %reduce-scatter.9.cloned.1.call-done = bf16[80,2560]{1,0:T(8,128)(2,1)} async-done(((bf16[1280,2560]{1,0:T(8,128)(2,1)}), bf16[80,2560]{1,0:T(8,128)(2,1)}) %reduce-scatter.9.cloned.1.call-update) | async-done | bytes 409616 | tf_op jit(solution)/shard_map/reduce_scatter | solution.py:132
  228.3 2.1 copy.80
  231.5 1.7 fusion.8
  233.6 63.2 %reduce-scatter.11.cloned.1.call-done = bf16[160,1280]{1,0:T(8,128)(2,1)} async-done(((bf16[2560,1280]{1,0:T(8,128)(2,1)}), bf16[160,1280]{1,0:T(8,128)(2,1)}) %reduce-scatter.11.cloned.1.call-update) | async-done | bytes 409616 | tf_op jit(solution)/shard_map/reduce_scatter | solution.py:135
  296.7 2.1 copy.82
  299.4 0.9 copy.64
  301.7 0.9 copy.66
  302.6 75.3 %psum.7 = f32[1280]{0:T(1024)S(1)} all-reduce(f32[1280]{0:T(1024)S(1)} %get-tuple-element.28), channel_id=1, replica_groups=mesh['seq'=16,'dp'=16] {'seq','dp'}, use_global_device_ids=true, to_apply=%region_17.18 | all-reduce | flops 1280 | bytes 10240 | tf_op jit(solution)/shard_map/psum | solution.py:148
  380.0 78.3 %reduce-scatter.15.cloned.1.call-done = bf16[80,160]{1,0:T(8,128)(2,1)} async-done(((bf16[1280,160]{1,0:T(8,128)(2,1)}), bf16[80,160]{1,0:T(8,128)(2,1)}) %reduce-scatter.15.cloned.1.call-update) | async-done | bytes 25616
  (97 shorter events, 16.9 us)
Async XLA Ops:
  7.2 14.3 %copy-start = (bf16[1,192,1280]{2,1,0:T(8,128)(2,1)S(1)}, bf16[1,192,1280]{2,1,0:T(8,128)(2,1)}, u32[]{:S(2)}) copy-start(bf16[1,192,1280]{2,1,0:T(8,128)(2,1)} %param.14) | copy-start | bytes 1474564
  7.2 75.5 %all-gather.5.cloned.1.call-start = ((), (), s32[]{:S(2)}) async-start(), calls=%async_computation.7 | async-start | bytes 6963200 | tf_op jit(solution)/shard_map/all_gather | solution.py:39
  7.9 143.1 %all-gather.3.cloned.1.call-start = ((), (), s32[]{:S(2)}) async-start(), calls=%async_computation.6 | async-start | bytes 6963200 | tf_op jit(solution)/shard_map/all_gather | solution.py:40
  12.9 16.1 %all-to-all-start = ((s32[16,1,32]{2,1,0:T(1,128)}), s32[16,1,32]{2,1,0:T(1,128)S(1)}, u32[]{:S(2)}, u32[]{:S(2)}) async-start(s32[16,1,32]{2,1,0:T(1,128)} %all_to_all.9), calls=%async_computation | async-start | bytes 16384 | tf_op jit(solution)/shard_map/all_to_all | solution.py:67
  29.0 3.9 copy-start.8
  29.0 4.1 copy-start.9
  29.0 50.7 %all-to-all-start.1 = ((bf16[16,32,1280]{2,1,0:T(8,128)(2,1)}), bf16[16,32,1280]{2,1,0:T(8,128)(2,1)S(1)}, u32[]{:S(2)}, u32[]{:S(2)}) async-start(bf16[16,32,1280]{2,1,0:T(8,128)(2,1)} %bitcast.13), calls=%async_computation.1 | async-start | bytes 2621440 | tf_op jit(solution)/shard_map/all_to_all | solution.py:60
  32.8 1.0 copy-start.10
  32.9 1.2 copy-start.14
  32.9 195.4 %reduce-scatter.9.cloned.1.call-start = ((), (), s32[]{:S(2)}) async-start(), calls=%async_computation.8 | async-start | bytes 6963200 | tf_op jit(solution)/shard_map/reduce_scatter | solution.py:132
  33.2 2.7 copy-start.3
  33.8 2.0 copy-start.11
  34.0 1.8 copy-start.1
  38.2 1.9 copy-start.15
  38.3 39.8 %copy-start.13 = (bf16[1,128,1280]{2,1,0:T(8,128)(2,1)S(1)}, bf16[1,128,1280]{2,1,0:T(8,128)(2,1)}, u32[]{:S(2)}) copy-start(bf16[1,128,1280]{2,1,0:T(8,128)(2,1)} %param.13) | copy-start | bytes 983044
  160.8 136.0 %reduce-scatter.11.cloned.1.call-start = ((), (), s32[]{:S(2)}) async-start(), calls=%async_computation.9 | async-start | bytes 6963200 | tf_op jit(solution)/shard_map/reduce_scatter | solution.py:135
  165.5 213.0 %reduce-scatter.13.cloned.1.call-start = ((), (), s32[]{:S(2)}) async-start(), calls=%async_computation.10 | async-start | bytes 696320
  230.4 228.0 %reduce-scatter.15.cloned.1.call-start = ((), (), s32[]{:S(2)}) async-start(), calls=%async_computation.11 | async-start | bytes 696320
  230.4 1.0 copy-start.7
  230.4 1.1 copy-start.12
  230.8 2.4 copy-start.5
  231.5 1.7 copy-start.4
  233.2 65.6 %copy-start.2 = (bf16[1,128,1280]{1,2,0:T(8,128)(2,1)S(1)}, bf16[1,128,1280]{1,2,0:T(8,128)(2,1)}, u32[]{:S(2)}) copy-start(bf16[1,128,1280]{1,2,0:T(8,128)(2,1)} %copy-done.1) | copy-start | bytes 983044
  298.9 2.3 copy-start.17
  (2 other events, 1.4 us)
Sparse Core Ops, SparseCore 0:
  10.4 70.4 all-gather.4
  83.3 67.5 all-gather.2
  160.9 67.3 reduce-scatter.8
  230.7 65.9 reduce-scatter.10
  300.1 76.7 reduce-scatter.12
  380.2 78.0 reduce-scatter.14
where the time goes:
time: 467 us
  waiting for transfers between devices  270 us (58%)
  blocking collectives  113 us (24%)
  matrix products  29.6 us (6%)
  local copies, waits for them, and re-layouts  21.1 us (5%)
  between operations  15.1 us (3%)
  starting transfers between devices  12.6 us (3%)
  other arithmetic  5.58 us (1%)
    unnamed x8, waiting for transfers between devices  79.8 us
    psum x1, blocking collectives, per_device(): gain_total = lax.psum(gain_term, ('seq', 'dp'))  75.3 us
    all_gather x1, waiting for transfers between devices, per_device(): lax.all_gather(w_down, 'dp', axis=0, tiled=True)  64.3 us
    reduce_scatter x1, waiting for transfers between devices, per_device(): lax.psum_scatter(down_term.astype(jnp.bfloat16), 'seq', scatter_dimension...  63.2 us
    reduce_scatter x1, waiting for transfers between devices, per_device(): lax.psum_scatter(up_term.astype(jnp.bfloat16), 'seq', scatter_dimension=0...  57.6 us
    unnamed x1, blocking collectives  37.7 us
    dot_general x4, matrix products, contract(): lax.dot_general(left, right, (((left_dim,), (right_dim,)), ((), ())), pre...  19.6 us
    unnamed x49, local copies, waits for them, and re-layouts  12.1 us
  transfers between devices with their start and end apart: 8, of which 5 were waited for; matrix products, arithmetic and copies ran while one was open for 9% of the time, Pallas kernels for 0%

commit v1 on v0

--- a/solution.py
+++ b/solution.py
@@ -3,11 +3,13 @@
 import jax.numpy as jnp
 from jax import lax
 from jax.sharding import PartitionSpec as P
+from jax.lax import all_gather
 
 HEADS = 16
 HDIM = 80
 BLK = 64
 PIECE = 16
+number_column_on = lambda raw: jnp.sum(all_gather(raw, ("seq", "dp")), 0)
 
 
 def contract(left, right, left_dim, right_dim):
@@ -145,7 +147,7 @@
         ).astype(jnp.float32),
     )
     factor = 1.0 / math.sqrt(data_count * seq_count * tokens)
-    gain_total = lax.psum(gain_term, ("seq", "dp"))
+    gain_total = number_column_on(gain_term)
     return (
         grad_query.reshape(1, tokens, feat_dim),
         grad_key.reshape(1, tokens, feat_dim),

time: 467 us -> 574 us (1.23)
  waiting for transfers between devices: 270 us -> 448 us
  blocking collectives: 113 us -> 37.8 us
    all_gather x0 -> x1, waiting for transfers between devices: none -> 99.6 us  [number_column_on = lambda raw: jnp.sum(all_gather(raw, ('seq', 'dp')), 0)]
    unnamed x8 -> x9, waiting for transfers between devices: 79.8 us -> 160 us
    psum x1 -> x0, blocking collectives: 75.3 us -> none  [per_device(): gain_total = lax.psum(gain_term, ('seq', 'dp'))]
    unnamed x49 -> x52, local copies, waits for them, and re-layouts: 12.1 us -> 14.1 us
  transfers between devices with their start and end apart: 8 -> 9, of which waited for: 5 -> 7; matrix products, arithmetic and copies ran while one was open for 9% -> 8% of each run, Pallas kernels for 0% -> 0%
where the time goes in v1:
time: 574 us; the launch traced here: 573 us
  waiting for transfers between devices  448 us (78%)
  blocking collectives  37.8 us (7%)
  matrix products  27.4 us (5%)
  local copies, waits for them, and re-layouts  23.8 us (4%)
  between operations  15.2 us (3%)
  starting transfers between devices  13.4 us (2%)
  other arithmetic  7.67 us (1%)
    unnamed x9, waiting for transfers between devices  160 us
    all_gather x1, waiting for transfers between devices, number_column_on = lambda raw: jnp.sum(all_gather(raw, ('seq', 'dp')), 0)  99.6 us
    all_gather x1, waiting for transfers between devices, per_device(): lax.all_gather(w_down, 'dp', axis=0, tiled=True)  63.9 us
    reduce_scatter x1, waiting for transfers between devices, per_device(): lax.psum_scatter(down_term.astype(jnp.bfloat16), 'seq', scatter_dimension...  62.8 us
    reduce_scatter x1, waiting for transfers between devices, per_device(): lax.psum_scatter(up_term.astype(jnp.bfloat16), 'seq', scatter_dimension=0...  56.9 us
    unnamed x1, blocking collectives  37.8 us
    dot_general x4, matrix products, contract(): lax.dot_general(left, right, (((left_dim,), (right_dim,)), ((), ())), pre...  19.6 us
    unnamed x52, local copies, waits for them, and re-layouts  14.1 us
  transfers between devices with their start and end apart: 9, of which 7 were waited for; matrix products, arithmetic and copies ran while one was open for 8% of the time, Pallas kernels for 0%

profile of v1, /device:TPU:2, one launch (start us, length us, event | category | flops | bytes accessed | tf_op | source)
XLA Modules:
  0.0 573.0 jit_solution(10131701487325854210)
XLA Ops:
  11.0 1.2 scatter_custom_fusion
  12.9 8.6 %all-to-all-start = ((s32[16,1,32]{2,1,0:T(1,128)}), s32[16,1,32]{2,1,0:T(1,128)S(1)}, u32[]{:S(2)}, u32[]{:S(2)}) async-start(s32[16,1,32]{2,1,0:T(1,128)} %all_to_all.9), calls=%async_computation | async-start | bytes 16384 | tf_op jit(solution)/shard_map/all_to_all | solution.py:69
  21.5 2.7 scatter_custom_fusion.1
  24.1 4.9 all-to-all-done
  29.0 4.5 all-to-all-start.1
  35.6 0.9 copy-done.17
  39.8 37.8 %all-reduce.1 = bf16[1280]{0:T(1024)(128)(2,1)S(1)} all-reduce(bf16[1280]{0:T(1024)(128)(2,1)S(1)} %dynamic-update-slice), channel_id=1, replica_groups=mesh['seq'=16,'dp'=16] {'dp'}, use_global_device_ids=true, to_apply=%add.1 | all-reduce | flops 1280 | bytes 5120
  79.4 3.7 scatter_custom_fusion.2
  83.1 3.9 fusion.31
  87.0 63.9 %all-gather.6.cloned.1.call-done = bf16[2560,1280]{1,0:T(8,128)(2,1)} async-done(((bf16[160,1280]{1,0:T(8,128)(2,1)}), bf16[2560,1280]{1,0:T(8,128)(2,1)}) %all-gather.6.cloned.1.call-update) | async-done | bytes 6553616 | tf_op jit(solution)/shard_map/all_gather | solution.py:42
  151.0 5.1 fusion.1
  156.1 4.7 convolution_convert_fusion.1
  160.8 4.6 convolution_convert_fusion
  165.5 5.2 multiply_reduce_fusion
  171.4 56.9 %reduce-scatter.9.cloned.1.call-done = bf16[80,2560]{1,0:T(8,128)(2,1)} async-done(((bf16[1280,2560]{1,0:T(8,128)(2,1)}), bf16[80,2560]{1,0:T(8,128)(2,1)}) %reduce-scatter.9.cloned.1.call-update) | async-done | bytes 409616 | tf_op jit(solution)/shard_map/reduce_scatter | solution.py:134
  228.3 2.1 copy.80
  232.0 1.7 fusion.8
  234.0 62.8 %reduce-scatter.11.cloned.1.call-done = bf16[160,1280]{1,0:T(8,128)(2,1)} async-done(((bf16[2560,1280]{1,0:T(8,128)(2,1)}), bf16[160,1280]{1,0:T(8,128)(2,1)}) %reduce-scatter.11.cloned.1.call-update) | async-done | bytes 409616 | tf_op jit(solution)/shard_map/reduce_scatter | solution.py:137
  296.7 2.1 copy.82
  299.4 0.9 copy.64
  302.6 99.6 %all-gather.10.cloned.1.call-done = f32[256,1,1280]{2,1,0:T(1,128)} async-done(((f32[1,1,1280]{2,1,0:T(1,128)}), f32[256,1,1280]{2,1,0:T(1,128)}) %all-gather.10.cloned.1.call-update) | async-done | bytes 1310736 | tf_op jit(solution)/shard_map/all_gather | solution.py:12
  402.2 2.1 reduce_sum.82
  404.9 78.1 %reduce-scatter.13.cloned.1.call-done = bf16[160,80]{1,0:T(8,128)(2,1)} async-done(((bf16[2560,80]{1,0:T(8,128)(2,1)}), bf16[160,80]{1,0:T(8,128)(2,1)}) %reduce-scatter.13.cloned.1.call-update) | async-done | bytes 25616
  484.5 80.1 %reduce-scatter.15.cloned.1.call-done = bf16[80,160]{1,0:T(8,128)(2,1)} async-done(((bf16[1280,160]{1,0:T(8,128)(2,1)}), bf16[80,160]{1,0:T(8,128)(2,1)}) %reduce-scatter.15.cloned.1.call-update) | async-done | bytes 25616
  (103 shorter events, 19.7 us)
Async XLA Ops:
  7.2 14.3 %copy-start = (bf16[1,192,1280]{2,1,0:T(8,128)(2,1)S(1)}, bf16[1,192,1280]{2,1,0:T(8,128)(2,1)}, u32[]{:S(2)}) copy-start(bf16[1,192,1280]{2,1,0:T(8,128)(2,1)} %param.14) | copy-start | bytes 1474564
  7.2 75.9 %all-gather.8.cloned.1.call-start = ((), (), s32[]{:S(2)}) async-start(), calls=%async_computation.7 | async-start | bytes 6963200 | tf_op jit(solution)/shard_map/all_gather | solution.py:41
  7.9 143.1 %all-gather.6.cloned.1.call-start = ((), (), s32[]{:S(2)}) async-start(), calls=%async_computation.6 | async-start | bytes 6963200 | tf_op jit(solution)/shard_map/all_gather | solution.py:42
  12.9 16.1 %all-to-all-start = ((s32[16,1,32]{2,1,0:T(1,128)}), s32[16,1,32]{2,1,0:T(1,128)S(1)}, u32[]{:S(2)}, u32[]{:S(2)}) async-start(s32[16,1,32]{2,1,0:T(1,128)} %all_to_all.9), calls=%async_computation | async-start | bytes 16384 | tf_op jit(solution)/shard_map/all_to_all | solution.py:69
  29.0 4.6 copy-start.8
  29.0 4.8 copy-start.9
  29.0 50.4 %all-to-all-start.1 = ((bf16[16,32,1280]{2,1,0:T(8,128)(2,1)}), bf16[16,32,1280]{2,1,0:T(8,128)(2,1)}, u32[]{:S(2)}, u32[]{:S(2)}) async-start(bf16[16,32,1280]{2,1,0:T(8,128)(2,1)} %bitcast.13), calls=%async_computation.1 | async-start | bytes 2621440 | tf_op jit(solution)/shard_map/all_to_all | solution.py:62
  33.5 1.0 copy-start.10
  33.5 1.2 copy-start.14
  33.6 194.7 %reduce-scatter.9.cloned.1.call-start = ((), (), s32[]{:S(2)}) async-start(), calls=%async_computation.8 | async-start | bytes 6963200 | tf_op jit(solution)/shard_map/reduce_scatter | solution.py:134
  33.8 1.7 copy-start.3
  34.5 1.1 copy-start.11
  37.7 1.9 copy-start.15
  37.7 40.0 %copy-start.13 = (bf16[1,128,1280]{2,1,0:T(8,128)(2,1)S(1)}, bf16[1,128,1280]{2,1,0:T(8,128)(2,1)}, u32[]{:S(2)}) copy-start(bf16[1,128,1280]{2,1,0:T(8,128)(2,1)} %param.13) | copy-start | bytes 983044
  160.8 136.0 %reduce-scatter.11.cloned.1.call-start = ((), (), s32[]{:S(2)}) async-start(), calls=%async_computation.9 | async-start | bytes 6963200 | tf_op jit(solution)/shard_map/reduce_scatter | solution.py:137
  165.5 236.7 %all-gather.10.cloned.1.call-start = ((), (), s32[]{:S(2)}) async-start(), calls=%async_computation.10 | async-start | bytes 1315840 | tf_op jit(solution)/shard_map/all_gather | solution.py:12
  171.3 311.7 %reduce-scatter.13.cloned.1.call-start = ((), (), s32[]{:S(2)}) async-start(), calls=%async_computation.11 | async-start | bytes 696320
  230.4 334.2 %reduce-scatter.15.cloned.1.call-start = ((), (), s32[]{:S(2)}) async-start(), calls=%async_computation.12 | async-start | bytes 696320
  230.5 1.0 copy-start.7
  230.8 2.8 copy-start.5
  230.8 1.1 copy-start.12
  232.0 1.7 copy-start.4
  233.6 65.2 %copy-start.2 = (bf16[1,128,1280]{1,2,0:T(8,128)(2,1)S(1)}, bf16[1,128,1280]{1,2,0:T(8,128)(2,1)}, u32[]{:S(2)}) copy-start(bf16[1,128,1280]{1,2,0:T(8,128)(2,1)} %copy-done.1) | copy-start | bytes 983044
  298.9 2.3 copy-start.18
  (4 other events, 3.2 us)
Sparse Core Ops, SparseCore 0:
  10.4 70.4 all-gather.7
  83.3 67.5 all-gather.5
  160.9 67.3 reduce-scatter.8
  230.7 65.9 reduce-scatter.10
  300.7 101.4 all-gather.9
  405.6 77.4 reduce-scatter.12
  486.5 78.0 reduce-scatter.14
